TPU v7x, 32 devices: a whole 2x2x4 slice. The times are simulated.
32 devices in a mesh: samp: 4 (over y, x), var: 8 (over z, core).
Axes of the slice: x: 2, y: 2, z: 4, core: 2. Of those that a mesh axis runs over, the one named last changes fastest.
Arguments:
- dosage: bfloat16 [8192, 16384], P('samp', 'var'), may hold values from -6 to 6
- traits: float32 [8192, 128], P(('samp', 'var')), may hold values from -6 to 6
- coef_now: float32 [128, 256, 128], P('var', 'samp'), may hold values from -6 to 6
- coef_prev: float32 [128, 256, 128], P('var', 'samp'), may hold values from -6 to 6
- block_inverse: bfloat16 [128, 256, 4, 256], P('var', 'samp'), may hold values from -0.1875 to 0.1875
- penalty: float32 [128], replicated, may hold values from 0.05 to 0.5
- block_start: int32 [64], replicated, may hold values from 0 to 1, as said below
- unit_owner: int32 [64], replicated, may hold values from 0 to 7, as said below
Outputs:
- coef_next: float32 [128, 256, 128], P('var', 'samp')
- residual: float32 [8192, 128], P(('samp', 'var'))
Inputs may be any that keep to these rules, and one draw needn't show every extreme that they name: `block_start`: 1 where a linkage block begins, else 0. The first unit of every device's 8 units begins a block, and a block holds 1 to 4 units of 256 variants. `unit_owner`: the index along var of the device that owns each unit's block, equal for all units of a block. For a unit of the device with index d along var it is (d + j) modulo the size of var, with 1 <= j <= 4. An owner holds at most 16 units and some owner holds exactly 16; the units of one device that belong to one owner are at most 4, and some device has exactly 4 for one owner.
All inputs are finite; a program needn't handle non-finite values.
Results may differ from a plain program's by a relative error of at most 0.0072.
Values may be sent and summed in bfloat16 or wider, within the bound.
No kernel may reach another device: no remote copies, remote signals or barrier semaphores. Data moves between devices by JAX's collectives and lax.ppermute only.
A program may use at most 64 MiB of HBM per device.

v0:
```python
import math
import jax
import jax.numpy as jnp
from jax import lax
from jax.sharding import PartitionSpec as P

MOMENTA = (0.4, 0.55)


def shifted(block, axis, distance):
    devices = range(lax.axis_size(axis))
    route = [((i - distance) % len(devices), i) for i in devices]
    return lax.ppermute(block, axis, route)


def unit_tables(block_start, unit_owner, per_device, owners):
    unit_count = block_start.shape[0]
    unit_ids = jnp.arange(unit_count, dtype=jnp.int32)
    shard_of = unit_ids // per_device
    owner_hot = (unit_owner[:, None] == jnp.arange(owners, dtype=jnp.int32)[None, :]).astype(
        jnp.int32
    )
    running = jnp.cumsum(owner_hot, axis=0) - owner_hot
    slot_index = jnp.sum(running * owner_hot, axis=1)
    first_unit = shard_of * per_device
    before_shard = jnp.sum(running[first_unit] * owner_hot, axis=1)
    pair_place = slot_index - before_shard
    block_begin = lax.cummax(jnp.where(block_start == 1, unit_ids, 0), axis=0)
    block_later = lax.cummin(
        jnp.where(block_start == 1, unit_ids, unit_count), axis=0, reverse=True
    )
    block_follow = jnp.concatenate([block_later[1:], jnp.full((1,), unit_count, jnp.int32)])
    block_length = block_follow - block_begin
    offset = unit_ids - block_begin
    return (shard_of, slot_index, pair_place, offset, block_length)


def shards(dosage, traits, coef_now, coef_prev, block_inverse, penalty, block_start, unit_owner):
    owners = lax.axis_size("var")
    quarters = lax.axis_size("samp")
    var_index = lax.axis_index("var")
    samp_index = lax.axis_index("samp")
    capacity = coef_now.shape[0]
    quarter_rows = coef_now.shape[1]
    right_cols = coef_now.shape[2]
    unit_rows = block_inverse.shape[3]
    block_most = block_inverse.shape[2]
    per_device = dosage.shape[1] // unit_rows
    pair_cap = min(block_most, per_device)
    reach = capacity // pair_cap
    samples = dosage.shape[0] * quarters
    variants = dosage.shape[1] * owners
    inv_scale = 1.0 / math.sqrt(variants)
    grad_scale = 0.5 / math.sqrt(samples)
    shard_of, slot_index, pair_place, offset, block_length = unit_tables(
        block_start, unit_owner, per_device, owners
    )
    owner_gap = (unit_owner - shard_of) % owners
    unit_code = (owner_gap - 1) * pair_cap + pair_place
    columns = jnp.arange(reach * pair_cap, dtype=jnp.int32)
    local_ids = var_index * per_device + jnp.arange(per_device, dtype=jnp.int32)
    local_code = unit_code[local_ids]
    matches = local_code[None, :] == columns[:, None]
    send_unit = jnp.sum(
        matches.astype(jnp.int32) * jnp.arange(per_device, dtype=jnp.int32)[None, :], axis=1
    )
    send_live = jnp.any(matches, axis=1)
    owned_flag = unit_owner == var_index
    slot_match = owned_flag[None, :] & (
        slot_index[None, :] == jnp.arange(capacity, dtype=jnp.int32)[:, None]
    )
    slot_hits = slot_match.astype(jnp.int32)
    slot_live = jnp.any(slot_match, axis=1)
    slot_code = jnp.sum(slot_hits * unit_code[None, :], axis=1)
    slot_offset = jnp.sum(slot_hits * offset[None, :], axis=1)
    slot_length = jnp.sum(slot_hits * block_length[None, :], axis=1)
    back_match = slot_live[None, :] & (slot_code[None, :] == columns[:, None])
    back_slot = jnp.sum(
        back_match.astype(jnp.int32) * jnp.arange(capacity, dtype=jnp.int32)[None, :], axis=1
    )
    back_live = jnp.any(back_match, axis=1)
    within = jnp.arange(block_most, dtype=jnp.int32)
    member_ids = jnp.clip(
        jnp.arange(capacity, dtype=jnp.int32)[:, None] - slot_offset[:, None] + within[None, :],
        0,
        capacity - 1,
    )
    member_live = (within[None, :] < slot_length[:, None]) & slot_live[:, None]
    panel_rows = block_inverse.reshape(capacity, quarter_rows, block_most * unit_rows)
    zero_half = jnp.zeros((), jnp.bfloat16)
    current, previous = (coef_now, coef_prev)
    residual = traits
    for momentum in MOMENTA:
        point = current + momentum * (current - previous)
        send_outgoing = jnp.where(
            back_live[:, None, None], point.astype(jnp.bfloat16)[back_slot], zero_half
        )
        send_outgoing = send_outgoing.reshape(reach, pair_cap, quarter_rows, right_cols)
        send_pieces = []
        for send_gap in range(1, reach + 1):
            send_pieces.append(shifted(send_outgoing[send_gap - 1], "var", -send_gap))
        send_received = jnp.stack(send_pieces).reshape(reach * pair_cap, quarter_rows, right_cols)
        local_rows = send_received[local_code]
        send_gathered = lax.all_gather(local_rows[:, None], "samp", axis=1, tiled=True)
        values = send_gathered.reshape(per_device * unit_rows, right_cols)
        summed = lax.psum_scatter(
            jnp.dot(dosage, values, preferred_element_type=jnp.float32) * inv_scale,
            "var",
            scatter_dimension=0,
            tiled=True,
        )
        residual = summed - traits
        residual_b = lax.all_gather(residual.astype(jnp.bfloat16), "var", axis=0, tiled=True)
        partial_grad = (
            lax.dot_general(
                dosage, residual_b, (((0,), (0,)), ((), ())), preferred_element_type=jnp.float32
            )
            * grad_scale
        )
        shaped = partial_grad.reshape(per_device, quarters, quarter_rows, right_cols)
        grad_sum = lax.psum(shaped, "samp")
        own_grad = lax.dynamic_index_in_dim(grad_sum, samp_index, 1, keepdims=False)
        outgoing = jnp.where(
            send_live[:, None, None], own_grad.astype(jnp.bfloat16)[send_unit], zero_half
        )
        outgoing = outgoing.reshape(reach, pair_cap, quarter_rows, right_cols)
        pieces = []
        for gap in range(1, reach + 1):
            pieces.append(shifted(outgoing[gap - 1], "var", gap))
        received = jnp.stack(pieces).reshape(reach * pair_cap, quarter_rows, right_cols)
        held_rows = jnp.where(slot_live[:, None, None], received[slot_code], zero_half)
        gathered = lax.all_gather(held_rows[:, None], "samp", axis=1, tiled=True)
        whole_grad = gathered.reshape(capacity, unit_rows, right_cols)
        block_grad = jnp.where(member_live[:, :, None, None], whole_grad[member_ids], zero_half)
        block_grad = block_grad.reshape(capacity, block_most * unit_rows, right_cols)
        direction = jnp.einsum(
            "irc,ick->irk", panel_rows, block_grad, preferred_element_type=jnp.float32
        )
        stepped = point - direction
        updated = jnp.sign(stepped) * jnp.maximum(jnp.abs(stepped) - penalty, 0.0)
        updated = jnp.where(slot_live[:, None, None], updated, jnp.float32(0.0))
        previous, current = (current, updated)
    return (current, residual)


def solution(mesh):
    placed = (
        P("samp", "var"),
        P(("samp", "var"), None),
        P("var", "samp", None),
        P("var", "samp", None),
        P("var", "samp", None, None),
        P(),
        P(),
        P(),
    )
    return jax.shard_map(
        shards,
        mesh=mesh,
        in_specs=placed,
        out_specs=(P("var", "samp", None), P(("samp", "var"), None)),
        check_vma=False,
    )
```

profile of v0, /device:TPU:0, one launch (start us, length us, event | category | flops | bytes accessed | tf_op | source)
XLA Modules:
  0.0 374.6 jit_solution(17077146969779160908)
XLA Ops:
  15.9 4.6 %collective-permute-start = (bf16[4,64,128]{2,1,0:T(8,128)(2,1)S(1)}, bf16[4,64,128]{2,1,0:T(8,128)(2,1)S(1)}, u32[]{:S(2)}, u32[]{:S(2)}) collective-permute-start(bf16[4,64,128]{2,1,0:T(8,128)(2,1)S(1)} %get-tuple-element.27), channel_id=1, source_target_pairs={{1,0},{2,1},{3,2},{4,3},{5,4},{6,5},{7,6},{0,7},{9,8},{10,9},{11,1... | collective-permute-start | bytes 196616 | tf_op jit(solution)/shard_map/ppermute | solution.py:13
  20.5 3.3 collective-permute-start.1
  27.7 11.3 %all-gather = bf16[8,256,128]{2,1,0:T(8,128)(2,1)S(1)} all-gather(bf16[8,64,128]{2,1,0:T(8,128)(2,1)S(1)} %gather_fusion.3), channel_id=2, replica_groups=mesh['samp'=4,'var'=8] {'samp'}, dimensions={1}, use_global_device_ids=true | all-gather | bytes 655360 | tf_op jit(solution)/shard_map/all_gather | solution.py:104
  39.0 7.4 %fusion.3 = f32[2048,128]{0,1:T(8,128)} fusion(bf16[2048,128]{1,0:T(8,128)(2,1)S(1)} %bitcast.106, bf16[2048,2048]{1,0:T(8,128)(2,1)} %param.8), kind=kOutput, calls=%fused_computation.21 | convolution fusion | flops 1074003968 | bytes 9961472 | tf_op jit(solution)/shard_map/dot_general | solution.py:107
  46.8 32.6 %reduce-scatter.3.cloned.1.call-done = f32[256,128]{0,1:T(8,128)} async-done(((f32[2048,128]{0,1:T(8,128)}), f32[256,128]{0,1:T(8,128)}) %reduce-scatter.3.cloned.1.call-update) | async-done | bytes 131088 | tf_op jit(solution)/shard_map/reduce_scatter | solution.py:106
  80.3 14.9 %all_gather.19 = bf16[2048,128]{0,1:T(8,128)(2,1)S(1)} all-gather(bf16[256,128]{0,1:T(8,128)(2,1)S(1)} %subtract_convert_fusion), channel_id=1, replica_groups=mesh['samp'=4,'var'=8] {'var'}, dimensions={0}, use_global_device_ids=true | all-gather | bytes 589824 | tf_op jit(solution)/shard_map/all_gather | solution.py:113
  95.3 4.7 %fusion.2 = f32[2048,128]{0,1:T(8,128)S(1)} fusion(bf16[2048,128]{0,1:T(8,128)(2,1)S(1)} %all_gather.19, bf16[2048,2048]{1,0:T(8,128)(2,1)} %param.8), kind=kOutput, calls=%fused_computation.19 | convolution fusion | flops 1074003968 | bytes 9961472 | tf_op jit(solution)/shard_map/dot_general | solution.py:115
  100.3 41.9 %all-reduce.2 = bf16[8,4,64,128]{3,2,1,0:T(8,128)(2,1)S(1)} all-reduce(f32[8,4,64,128]{3,2,1,0:T(8,128)S(1)} %bitcast.104), channel_id=1, replica_groups=mesh['samp'=4,'var'=8] {'samp'}, use_global_device_ids=true, to_apply=%region_12.13 | all-reduce | flops 262144 | bytes 1572864 | tf_op jit(solution)/shard_map/psum | solution.py:121
  148.6 4.5 %collective-permute-done.7 = bf16[4,64,128]{2,1,0:T(8,128)(2,1)S(1)} collective-permute-done((bf16[4,64,128]{2,1,0:T(8,128)(2,1)S(1)}, bf16[4,64,128]{2,1,0:T(8,128)(2,1)S(1)}, u32[]{:S(2)}, u32[]{:S(2)}) %collective-permute-start.7) | collective-permute-done | bytes 65568 | tf_op jit(solution)/shard_map/ppermute | solution.py:13
  155.1 3.2 reshape.362
  158.3 20.1 %all-gather.5.cloned.1.call-done = bf16[16,4,64,128]{3,2,1,0:T(8,128)(2,1)} async-done(((bf16[16,1,64,128]{3,2,1,0:T(8,128)(2,1)}), bf16[16,4,64,128]{3,2,1,0:T(8,128)(2,1)}) %all-gather.5.cloned.1.call-update) | async-done | bytes 1048592 | tf_op jit(solution)/shard_map/all_gather | solution.py:132
  178.5 4.2 %gather_fusion.6 = bf16[64,256,128]{2,1,0:T(8,128)(2,1)} fusion(bf16[16,256,128]{2,1,0:T(8,128)(2,1)} %bitcast.100, s32[1024]{0:T(1024)S(1)} %pad_clamp_fusion), kind=kCustom, calls=%fused_computation.6 | custom fusion | bytes 8388864 | tf_op jit(solution)/shard_map/gather | solution.py:134
  182.7 6.2 %bitcast_select_fusion.1 = bf16[16,1024,128]{2,1,0:T(8,128)(2,1)S(1)} fusion(pred[16,1024]{1,0:T(8,128)(4,1)S(1)} %bitcast.112, bf16[16,1024,128]{2,1,0:T(8,128)(2,1)} %bitcast.103), kind=kLoop, calls=%fused_computation.13 | loop fusion | flops 2097152 | bytes 8404992 | tf_op jit(solution)/shard_map/jit(_where)/select_n | solution.py:134
  194.3 3.3 collective-permute-start.9
  201.3 11.5 %all-gather.1 = bf16[8,256,128]{2,1,0:T(8,128)(2,1)S(1)} all-gather(bf16[8,64,128]{2,1,0:T(8,128)(2,1)S(1)} %gather_fusion.8), channel_id=3, replica_groups=mesh['samp'=4,'var'=8] {'samp'}, dimensions={1}, use_global_device_ids=true | all-gather | bytes 655360 | tf_op jit(solution)/shard_map/all_gather | solution.py:104
  212.9 7.3 %fusion.1 = f32[2048,128]{0,1:T(8,128)} fusion(bf16[2048,128]{1,0:T(8,128)(2,1)S(1)} %bitcast.107, bf16[2048,2048]{1,0:T(8,128)(2,1)} %param.8), kind=kOutput, calls=%fused_computation.17 | convolution fusion | flops 1074003968 | bytes 9961472 | tf_op jit(solution)/shard_map/dot_general | solution.py:107
  220.2 33.1 %reduce-scatter.5.cloned.1.call-done = f32[256,128]{0,1:T(8,128)} async-done(((f32[2048,128]{0,1:T(8,128)}), f32[256,128]{0,1:T(8,128)}) %reduce-scatter.5.cloned.1.call-update) | async-done | bytes 131088 | tf_op jit(solution)/shard_map/reduce_scatter | solution.py:106
  254.2 14.9 %all_gather.22 = bf16[2048,128]{0,1:T(8,128)(2,1)S(1)} all-gather(bf16[256,128]{0,1:T(8,128)(2,1)S(1)} %get-tuple-element.13), channel_id=1, replica_groups=mesh['samp'=4,'var'=8] {'var'}, dimensions={0}, use_global_device_ids=true | all-gather | bytes 589824 | tf_op jit(solution)/shard_map/all_gather | solution.py:113
  269.2 5.7 %fusion = f32[2048,128]{0,1:T(8,128)} fusion(bf16[2048,128]{0,1:T(8,128)(2,1)S(1)} %all_gather.22, bf16[2048,2048]{1,0:T(8,128)(2,1)} %param.8), kind=kOutput, calls=%fused_computation.15 | convolution fusion | flops 1074003968 | bytes 9961472 | tf_op jit(solution)/shard_map/dot_general | solution.py:115
  276.4 42.3 %all-reduce.3 = bf16[8,4,64,128]{3,2,1,0:T(8,128)(2,1)} all-reduce(f32[8,4,64,128]{3,2,1,0:T(8,128)S(1)} %bitcast.105), channel_id=1, replica_groups=mesh['samp'=4,'var'=8] {'samp'}, use_global_device_ids=true, to_apply=%region_16.17 | all-reduce | flops 262144 | bytes 1572864 | tf_op jit(solution)/shard_map/psum | solution.py:121
  326.0 4.5 %collective-permute-done.15 = bf16[4,64,128]{2,1,0:T(8,128)(2,1)S(1)} collective-permute-done((bf16[4,64,128]{2,1,0:T(8,128)(2,1)S(1)}, bf16[4,64,128]{2,1,0:T(8,128)(2,1)S(1)}, u32[]{:S(2)}, u32[]{:S(2)}) %collective-permute-start.15) | collective-permute-done | bytes 65568 | tf_op jit(solution)/shard_map/ppermute | solution.py:13
  332.8 23.1 %all-gather.7.cloned.1.call-done = bf16[16,4,64,128]{3,2,1,0:T(8,128)(2,1)} async-done(((bf16[16,1,64,128]{3,2,1,0:T(8,128)(2,1)}), bf16[16,4,64,128]{3,2,1,0:T(8,128)(2,1)}) %all-gather.7.cloned.1.call-update) | async-done | bytes 1048592 | tf_op jit(solution)/shard_map/all_gather | solution.py:132
  355.9 4.2 %gather_fusion.11 = bf16[64,256,128]{2,1,0:T(8,128)(2,1)} fusion(bf16[16,256,128]{2,1,0:T(8,128)(2,1)} %bitcast.101, s32[1024]{0:T(1024)S(1)} %pad_clamp_fusion), kind=kCustom, calls=%fused_computation.11 | custom fusion | bytes 8388864 | tf_op jit(solution)/shard_map/gather | solution.py:134
  360.1 6.1 %bitcast_select_fusion = bf16[16,1024,128]{2,1,0:T(8,128)(2,1)S(1)} fusion(pred[16,1024]{1,0:T(8,128)(4,1)S(1)} %bitcast.113, bf16[16,1024,128]{2,1,0:T(8,128)(2,1)} %bitcast.102), kind=kLoop, calls=%fused_computation.12 | loop fusion | flops 2097152 | bytes 8404992 | tf_op jit(solution)/shard_map/jit(_where)/select_n | solution.py:134
  (118 shorter events, 45.2 us)
Async XLA Ops:
  7.2 72.2 %reduce-scatter.3.cloned.1.call-start = ((), (), s32[]{:S(2)}) async-start(), calls=%async_computation.2 | async-start | bytes 1179648 | tf_op jit(solution)/shard_map/reduce_scatter | solution.py:106
  15.9 8.6 %collective-permute-start = (bf16[4,64,128]{2,1,0:T(8,128)(2,1)S(1)}, bf16[4,64,128]{2,1,0:T(8,128)(2,1)S(1)}, u32[]{:S(2)}, u32[]{:S(2)}) collective-permute-start(bf16[4,64,128]{2,1,0:T(8,128)(2,1)S(1)} %get-tuple-element.27), channel_id=1, source_target_pairs={{1,0},{2,1},{3,2},{4,3},{5,4},{6,5},{7,6},{0,7},{9,8},{10,9},{11,1... | collective-permute-start | bytes 196616 | tf_op jit(solution)/shard_map/ppermute | solution.py:13
  20.5 6.6 %collective-permute-start.3 = (bf16[4,64,128]{2,1,0:T(8,128)(2,1)S(1)}, bf16[4,64,128]{2,1,0:T(8,128)(2,1)S(1)}, u32[]{:S(2)}, u32[]{:S(2)}) collective-permute-start(bf16[4,64,128]{2,1,0:T(8,128)(2,1)S(1)} %get-tuple-element.28), channel_id=1, source_target_pairs={{4,0},{5,1},{6,2},{7,3},{0,4},{1,5},{2,6},{3,7},{12,8},{13,9},{14,... | collective-permute-start | bytes 196616 | tf_op jit(solution)/shard_map/ppermute | solution.py:13
  20.5 6.6 %collective-permute-start.2 = (bf16[4,64,128]{2,1,0:T(8,128)(2,1)S(1)}, bf16[4,64,128]{2,1,0:T(8,128)(2,1)S(1)}, u32[]{:S(2)}, u32[]{:S(2)}) collective-permute-start(bf16[4,64,128]{2,1,0:T(8,128)(2,1)S(1)} %get-tuple-element.29), channel_id=1, source_target_pairs={{3,0},{4,1},{5,2},{6,3},{7,4},{0,5},{1,6},{2,7},{11,8},{12,9},{13,... | collective-permute-start | bytes 196616 | tf_op jit(solution)/shard_map/ppermute | solution.py:13
  20.5 6.6 %collective-permute-start.1 = (bf16[4,64,128]{2,1,0:T(8,128)(2,1)S(1)}, bf16[4,64,128]{2,1,0:T(8,128)(2,1)S(1)}, u32[]{:S(2)}, u32[]{:S(2)}) collective-permute-start(bf16[4,64,128]{2,1,0:T(8,128)(2,1)S(1)} %get-tuple-element.30), channel_id=1, source_target_pairs={{2,0},{3,1},{4,2},{5,3},{6,4},{7,5},{0,6},{1,7},{10,8},{11,9},{12,... | collective-permute-start | bytes 196616 | tf_op jit(solution)/shard_map/ppermute | solution.py:13
  39.0 7.4 %copy-start.3 = (f32[256,128]{1,0:T(8,128)S(1)}, f32[256,128]{1,0:T(8,128)}, u32[]{:S(2)}) copy-start(f32[256,128]{1,0:T(8,128)} %param.9) | copy-start | bytes 393220
  46.4 132.1 %all-gather.5.cloned.1.call-start = ((), (), s32[]{:S(2)}) async-start(), calls=%async_computation.3 | async-start | bytes 1310720 | tf_op jit(solution)/shard_map/all_gather | solution.py:132
  143.0 5.6 %collective-permute-start.4 = (bf16[4,64,128]{2,1,0:T(8,128)(2,1)S(1)}, bf16[4,64,128]{2,1,0:T(8,128)(2,1)S(1)}, u32[]{:S(2)}, u32[]{:S(2)}) collective-permute-start(bf16[4,64,128]{2,1,0:T(8,128)(2,1)S(1)} %get-tuple-element.23), channel_id=1, source_target_pairs={{7,0},{0,1},{1,2},{2,3},{3,4},{4,5},{5,6},{6,7},{15,8},{8,9},{9,10... | collective-permute-start | bytes 196616 | tf_op jit(solution)/shard_map/ppermute | solution.py:13
  143.1 10.1 %collective-permute-start.7 = (bf16[4,64,128]{2,1,0:T(8,128)(2,1)S(1)}, bf16[4,64,128]{2,1,0:T(8,128)(2,1)S(1)}, u32[]{:S(2)}, u32[]{:S(2)}) collective-permute-start(bf16[4,64,128]{2,1,0:T(8,128)(2,1)S(1)} %get-tuple-element.24), channel_id=1, source_target_pairs={{4,0},{5,1},{6,2},{7,3},{0,4},{1,5},{2,6},{3,7},{12,8},{13,9},{14,... | collective-permute-start | bytes 196616 | tf_op jit(solution)/shard_map/ppermute | solution.py:13
  143.8 9.4 %collective-permute-start.6 = (bf16[4,64,128]{2,1,0:T(8,128)(2,1)S(1)}, bf16[4,64,128]{2,1,0:T(8,128)(2,1)S(1)}, u32[]{:S(2)}, u32[]{:S(2)}) collective-permute-start(bf16[4,64,128]{2,1,0:T(8,128)(2,1)S(1)} %get-tuple-element.25), channel_id=1, source_target_pairs={{5,0},{6,1},{7,2},{0,3},{1,4},{2,5},{3,6},{4,7},{13,8},{14,9},{15,... | collective-permute-start | bytes 196616 | tf_op jit(solution)/shard_map/ppermute | solution.py:13
  146.9 6.3 %collective-permute-start.5 = (bf16[4,64,128]{2,1,0:T(8,128)(2,1)S(1)}, bf16[4,64,128]{2,1,0:T(8,128)(2,1)S(1)}, u32[]{:S(2)}, u32[]{:S(2)}) collective-permute-start(bf16[4,64,128]{2,1,0:T(8,128)(2,1)S(1)} %get-tuple-element.26), channel_id=1, source_target_pairs={{6,0},{7,1},{0,2},{1,3},{2,4},{3,5},{4,6},{5,7},{14,8},{15,9},{8,1... | collective-permute-start | bytes 196616 | tf_op jit(solution)/shard_map/ppermute | solution.py:13
  154.7 98.7 %reduce-scatter.5.cloned.1.call-start = ((), (), s32[]{:S(2)}) async-start(), calls=%async_computation.4 | async-start | bytes 1179648 | tf_op jit(solution)/shard_map/reduce_scatter | solution.py:106
  182.7 6.2 %copy-start = (f32[16,64,128]{2,1,0:T(8,128)S(1)}, f32[16,64,128]{2,1,0:T(8,128)}, u32[]{:S(2)}) copy-start(f32[16,64,128]{2,1,0:T(8,128)} %param.10) | copy-start | bytes 1572868
  182.7 6.2 %copy-start.1 = (f32[16,64,128]{2,1,0:T(8,128)S(1)}, f32[16,64,128]{2,1,0:T(8,128)}, u32[]{:S(2)}) copy-start(f32[16,64,128]{2,1,0:T(8,128)} %param.11) | copy-start | bytes 1572868
  182.7 6.2 %copy-start.4 = (f32[128]{0:T(128)S(1)}, f32[128]{0:T(128)}, u32[]{:S(2)}) copy-start(f32[128]{0:T(128)} %param.13) | copy-start | bytes 1540
  191.5 6.1 %collective-permute-start.8 = (bf16[4,64,128]{2,1,0:T(8,128)(2,1)S(1)}, bf16[4,64,128]{2,1,0:T(8,128)(2,1)S(1)}, u32[]{:S(2)}, u32[]{:S(2)}) collective-permute-start(bf16[4,64,128]{2,1,0:T(8,128)(2,1)S(1)} %get-tuple-element.19), channel_id=1, source_target_pairs={{1,0},{2,1},{3,2},{4,3},{5,4},{6,5},{7,6},{0,7},{9,8},{10,9},{11,1... | collective-permute-start | bytes 196616 | tf_op jit(solution)/shard_map/ppermute | solution.py:13
  194.1 6.6 %collective-permute-start.11 = (bf16[4,64,128]{2,1,0:T(8,128)(2,1)S(1)}, bf16[4,64,128]{2,1,0:T(8,128)(2,1)S(1)}, u32[]{:S(2)}, u32[]{:S(2)}) collective-permute-start(bf16[4,64,128]{2,1,0:T(8,128)(2,1)S(1)} %get-tuple-element.20), channel_id=1, source_target_pairs={{4,0},{5,1},{6,2},{7,3},{0,4},{1,5},{2,6},{3,7},{12,8},{13,9},{14,... | collective-permute-start | bytes 196616 | tf_op jit(solution)/shard_map/ppermute | solution.py:13
  194.1 6.6 %collective-permute-start.10 = (bf16[4,64,128]{2,1,0:T(8,128)(2,1)S(1)}, bf16[4,64,128]{2,1,0:T(8,128)(2,1)S(1)}, u32[]{:S(2)}, u32[]{:S(2)}) collective-permute-start(bf16[4,64,128]{2,1,0:T(8,128)(2,1)S(1)} %get-tuple-element.21), channel_id=1, source_target_pairs={{3,0},{4,1},{5,2},{6,3},{7,4},{0,5},{1,6},{2,7},{11,8},{12,9},{13,... | collective-permute-start | bytes 196616 | tf_op jit(solution)/shard_map/ppermute | solution.py:13
  194.3 6.4 %collective-permute-start.9 = (bf16[4,64,128]{2,1,0:T(8,128)(2,1)S(1)}, bf16[4,64,128]{2,1,0:T(8,128)(2,1)S(1)}, u32[]{:S(2)}, u32[]{:S(2)}) collective-permute-start(bf16[4,64,128]{2,1,0:T(8,128)(2,1)S(1)} %get-tuple-element.22), channel_id=1, source_target_pairs={{2,0},{3,1},{4,2},{5,3},{6,4},{7,5},{0,6},{1,7},{10,8},{11,9},{12,... | collective-permute-start | bytes 196616 | tf_op jit(solution)/shard_map/ppermute | solution.py:13
  220.2 135.7 %all-gather.7.cloned.1.call-start = ((), (), s32[]{:S(2)}) async-start(), calls=%async_computation.5 | async-start | bytes 1310720 | tf_op jit(solution)/shard_map/all_gather | solution.py:132
  320.4 5.6 %collective-permute-start.12 = (bf16[4,64,128]{2,1,0:T(8,128)(2,1)S(1)}, bf16[4,64,128]{2,1,0:T(8,128)(2,1)S(1)}, u32[]{:S(2)}, u32[]{:S(2)}) collective-permute-start(bf16[4,64,128]{2,1,0:T(8,128)(2,1)S(1)} %get-tuple-element.15), channel_id=1, source_target_pairs={{7,0},{0,1},{1,2},{2,3},{3,4},{4,5},{5,6},{6,7},{15,8},{8,9},{9,10... | collective-permute-start | bytes 196616 | tf_op jit(solution)/shard_map/ppermute | solution.py:13
  320.5 10.1 %collective-permute-start.15 = (bf16[4,64,128]{2,1,0:T(8,128)(2,1)S(1)}, bf16[4,64,128]{2,1,0:T(8,128)(2,1)S(1)}, u32[]{:S(2)}, u32[]{:S(2)}) collective-permute-start(bf16[4,64,128]{2,1,0:T(8,128)(2,1)S(1)} %get-tuple-element.16), channel_id=1, source_target_pairs={{4,0},{5,1},{6,2},{7,3},{0,4},{1,5},{2,6},{3,7},{12,8},{13,9},{14,... | collective-permute-start | bytes 196616 | tf_op jit(solution)/shard_map/ppermute | solution.py:13
  321.2 9.4 %collective-permute-start.14 = (bf16[4,64,128]{2,1,0:T(8,128)(2,1)S(1)}, bf16[4,64,128]{2,1,0:T(8,128)(2,1)S(1)}, u32[]{:S(2)}, u32[]{:S(2)}) collective-permute-start(bf16[4,64,128]{2,1,0:T(8,128)(2,1)S(1)} %get-tuple-element.17), channel_id=1, source_target_pairs={{5,0},{6,1},{7,2},{0,3},{1,4},{2,5},{3,6},{4,7},{13,8},{14,9},{15,... | collective-permute-start | bytes 196616 | tf_op jit(solution)/shard_map/ppermute | solution.py:13
  324.3 6.3 %collective-permute-start.13 = (bf16[4,64,128]{2,1,0:T(8,128)(2,1)S(1)}, bf16[4,64,128]{2,1,0:T(8,128)(2,1)S(1)}, u32[]{:S(2)}, u32[]{:S(2)}) collective-permute-start(bf16[4,64,128]{2,1,0:T(8,128)(2,1)S(1)} %get-tuple-element.18), channel_id=1, source_target_pairs={{6,0},{7,1},{0,2},{1,3},{2,4},{3,5},{4,6},{5,7},{14,8},{15,9},{8,1... | collective-permute-start | bytes 196616 | tf_op jit(solution)/shard_map/ppermute | solution.py:13
  (1 other events, 6.1 us)
Sparse Core Ops, SparseCore 0:
  46.5 32.8 reduce-scatter.2
  154.8 23.6 all-gather.4
  220.3 32.9 reduce-scatter.4
  332.2 23.6 all-gather.6
where the time goes:
time: 375 us
  blocking collectives  137 us (37%)
  waiting for transfers between devices  127 us (34%)
  matrix products  28.7 us (8%)
  other arithmetic  23.6 us (6%)
  starting transfers between devices  21.9 us (6%)
  local copies, waits for them, and re-layouts  21.9 us (6%)
  between operations  14.2 us (4%)
    psum x2, blocking collectives, shards(): grad_sum = lax.psum(shaped, 'samp')  84.2 us
    reduce_scatter x2, waiting for transfers between devices, shards(): lax.psum_scatter(jnp.dot(dosage, values, preferred_element_type=jnp.float...  65.7 us
    all_gather x2, waiting for transfers between devices, shards(): gathered = lax.all_gather(held_rows[:, None], 'samp', axis=1, tiled=True)  43.2 us
    all_gather x2, blocking collectives, shards(): lax.all_gather(residual.astype(jnp.bfloat16), 'var', axis=0, tiled=True)  29.9 us
    all_gather x2, blocking collectives, shards(): lax.all_gather(local_rows[:, None], 'samp', axis=1, tiled=True)  22.8 us
    ppermute x16, starting transfers between devices, shifted(): return lax.ppermute(block, axis, route)  21.8 us
    ppermute x16, waiting for transfers between devices, shifted(): return lax.ppermute(block, axis, route)  18.3 us
    dot_general x2, matrix products, shards(): jnp.dot(dosage, values, preferred_element_type=jnp.float32) * inv_scale  14.7 us
  transfers between devices with their start and end apart: 20, of which 12 were waited for; matrix products, arithmetic and copies ran while one was open for 1% of the time, Pallas kernels for 0%

commit v1 on v0

--- a/solution.py
+++ b/solution.py
@@ -118,7 +118,7 @@
             * grad_scale
         )
         shaped = partial_grad.reshape(per_device, quarters, quarter_rows, right_cols)
-        grad_sum = lax.psum(shaped, "samp")
+        grad_sum = jnp.sum(lax.all_gather(shaped, "samp"), axis=0)
         own_grad = lax.dynamic_index_in_dim(grad_sum, samp_index, 1, keepdims=False)
         outgoing = jnp.where(
             send_live[:, None, None], own_grad.astype(jnp.bfloat16)[send_unit], zero_half

time: 375 us -> 402 us (1.072)
  waiting for transfers between devices: 127 us -> 232 us
  blocking collectives: 137 us -> 52.7 us
  other arithmetic: 23.6 us -> 29 us
    all_gather x0 -> x2, waiting for transfers between devices: none -> 102 us  [shards(): grad_sum = jnp.sum(lax.all_gather(shaped, 'samp'), axis=0)]
    psum x2 -> x0, blocking collectives: 84.2 us -> none  [shards(): grad_sum = lax.psum(shaped, 'samp')]
    reduce_sum x0 -> x2, other arithmetic: none -> 5.38 us  [shards(): grad_sum = jnp.sum(lax.all_gather(shaped, 'samp'), axis=0)]
  transfers between devices with their start and end apart: 20 -> 22, of which waited for: 12 -> 14; matrix products, arithmetic and copies ran while one was open for 1% -> 1% of each run, Pallas kernels for 0% -> 0%
where the time goes in v1:
time: 402 us; the launch traced here: 401 us
  waiting for transfers between devices  232 us (58%)
  blocking collectives  52.7 us (13%)
  other arithmetic  29 us (7%)
  matrix products  27.7 us (7%)
  starting transfers between devices  23.2 us (6%)
  local copies, waits for them, and re-layouts  21.8 us (5%)
  between operations  14.5 us (4%)
    all_gather x2, waiting for transfers between devices, shards(): grad_sum = jnp.sum(lax.all_gather(shaped, 'samp'), axis=0)  102 us
    reduce_scatter x2, waiting for transfers between devices, shards(): lax.psum_scatter(jnp.dot(dosage, values, preferred_element_type=jnp.float...  66 us
    all_gather x2, waiting for transfers between devices, shards(): gathered = lax.all_gather(held_rows[:, None], 'samp', axis=1, tiled=True)  44.8 us
    all_gather x2, blocking collectives, shards(): lax.all_gather(residual.astype(jnp.bfloat16), 'var', axis=0, tiled=True)  29.9 us
    ppermute x16, starting transfers between devices, shifted(): return lax.ppermute(block, axis, route)  23 us
    all_gather x2, blocking collectives, shards(): lax.all_gather(local_rows[:, None], 'samp', axis=1, tiled=True)  22.8 us
    ppermute x16, waiting for transfers between devices, shifted(): return lax.ppermute(block, axis, route)  19.9 us
    dot_general x2, matrix products, shards(): jnp.dot(dosage, values, preferred_element_type=jnp.float32) * inv_scale  14.7 us
  transfers between devices with their start and end apart: 22, of which 14 were waited for; matrix products, arithmetic and copies ran while one was open for 1% of the time, Pallas kernels for 0%

profile of v1, /device:TPU:0, one launch (start us, length us, event | category | flops | bytes accessed | tf_op | source)
XLA Modules:
  0.0 401.3 jit_solution(13274450160256288676)
XLA Ops:
  15.9 4.6 %collective-permute-start = (bf16[4,64,128]{2,1,0:T(8,128)(2,1)S(1)}, bf16[4,64,128]{2,1,0:T(8,128)(2,1)S(1)}, u32[]{:S(2)}, u32[]{:S(2)}) collective-permute-start(bf16[4,64,128]{2,1,0:T(8,128)(2,1)S(1)} %get-tuple-element.29), channel_id=1, source_target_pairs={{1,0},{2,1},{3,2},{4,3},{5,4},{6,5},{7,6},{0,7},{9,8},{10,9},{11,1... | collective-permute-start | bytes 196616 | tf_op jit(solution)/shard_map/ppermute | solution.py:13
  20.5 3.3 collective-permute-start.1
  27.7 11.3 %all-gather = bf16[8,256,128]{2,1,0:T(8,128)(2,1)S(1)} all-gather(bf16[8,64,128]{2,1,0:T(8,128)(2,1)S(1)} %gather_fusion.3), channel_id=2, replica_groups=mesh['samp'=4,'var'=8] {'samp'}, dimensions={1}, use_global_device_ids=true | all-gather | bytes 655360 | tf_op jit(solution)/shard_map/all_gather | solution.py:104
  39.0 7.4 %fusion.3 = f32[2048,128]{0,1:T(8,128)} fusion(bf16[2048,128]{1,0:T(8,128)(2,1)S(1)} %bitcast.106, bf16[2048,2048]{1,0:T(8,128)(2,1)} %param.8), kind=kOutput, calls=%fused_computation.21 | convolution fusion | flops 1074003968 | bytes 9961472 | tf_op jit(solution)/shard_map/dot_general | solution.py:107
  46.6 32.8 %reduce-scatter.3.cloned.1.call-done = f32[256,128]{0,1:T(8,128)} async-done(((f32[2048,128]{0,1:T(8,128)}), f32[256,128]{0,1:T(8,128)}) %reduce-scatter.3.cloned.1.call-update) | async-done | bytes 131088 | tf_op jit(solution)/shard_map/reduce_scatter | solution.py:106
  80.3 14.9 %all_gather.25 = bf16[2048,128]{0,1:T(8,128)(2,1)S(1)} all-gather(bf16[256,128]{0,1:T(8,128)(2,1)S(1)} %subtract_convert_fusion), channel_id=1, replica_groups=mesh['samp'=4,'var'=8] {'var'}, dimensions={0}, use_global_device_ids=true | all-gather | bytes 589824 | tf_op jit(solution)/shard_map/all_gather | solution.py:113
  95.3 4.7 %fusion.2 = f32[2048,128]{0,1:T(8,128)S(1)} fusion(bf16[2048,128]{0,1:T(8,128)(2,1)S(1)} %all_gather.25, bf16[2048,2048]{1,0:T(8,128)(2,1)} %param.8), kind=kOutput, calls=%fused_computation.19 | convolution fusion | flops 1074003968 | bytes 9961472 | tf_op jit(solution)/shard_map/dot_general | solution.py:115
  101.6 50.7 %all-gather.7.cloned.1.call-done = f32[4,8,4,64,128]{4,3,2,1,0:T(8,128)} async-done(((f32[1,8,4,64,128]{4,3,2,1,0:T(8,128)}), f32[4,8,4,64,128]{4,3,2,1,0:T(8,128)}) %all-gather.7.cloned.1.call-update) | async-done | bytes 4194320 | tf_op jit(solution)/shard_map/all_gather | solution.py:121
  161.4 4.9 %collective-permute-done.7 = bf16[4,64,128]{2,1,0:T(8,128)(2,1)S(1)} collective-permute-done((bf16[4,64,128]{2,1,0:T(8,128)(2,1)S(1)}, bf16[4,64,128]{2,1,0:T(8,128)(2,1)S(1)}, u32[]{:S(2)}, u32[]{:S(2)}) %collective-permute-start.7) | collective-permute-done | bytes 65568 | tf_op jit(solution)/shard_map/ppermute | solution.py:13
  169.2 3.2 reshape.355
  172.5 20.9 %all-gather.9.cloned.1.call-done = bf16[16,4,64,128]{3,2,1,0:T(8,128)(2,1)} async-done(((bf16[16,1,64,128]{3,2,1,0:T(8,128)(2,1)}), bf16[16,4,64,128]{3,2,1,0:T(8,128)(2,1)}) %all-gather.9.cloned.1.call-update) | async-done | bytes 1048592 | tf_op jit(solution)/shard_map/all_gather | solution.py:132
  193.4 4.2 %gather_fusion.6 = bf16[64,256,128]{2,1,0:T(8,128)(2,1)} fusion(bf16[16,256,128]{2,1,0:T(8,128)(2,1)} %bitcast.100, s32[1024]{0:T(1024)S(1)} %pad_clamp_fusion), kind=kCustom, calls=%fused_computation.6 | custom fusion | bytes 8388864 | tf_op jit(solution)/shard_map/gather | solution.py:134
  197.7 6.2 %bitcast_select_fusion.1 = bf16[16,1024,128]{2,1,0:T(8,128)(2,1)S(1)} fusion(pred[16,1024]{1,0:T(8,128)(4,1)S(1)} %bitcast.112, bf16[16,1024,128]{2,1,0:T(8,128)(2,1)} %bitcast.103), kind=kLoop, calls=%fused_computation.13 | loop fusion | flops 2097152 | bytes 8404992 | tf_op jit(solution)/shard_map/jit(_where)/select_n | solution.py:134
  209.2 3.3 collective-permute-start.9
  216.3 11.5 %all-gather.1 = bf16[8,256,128]{2,1,0:T(8,128)(2,1)S(1)} all-gather(bf16[8,64,128]{2,1,0:T(8,128)(2,1)S(1)} %gather_fusion.8), channel_id=3, replica_groups=mesh['samp'=4,'var'=8] {'samp'}, dimensions={1}, use_global_device_ids=true | all-gather | bytes 655360 | tf_op jit(solution)/shard_map/all_gather | solution.py:104
  227.8 7.3 %fusion.1 = f32[2048,128]{0,1:T(8,128)} fusion(bf16[2048,128]{1,0:T(8,128)(2,1)S(1)} %bitcast.107, bf16[2048,2048]{1,0:T(8,128)(2,1)} %param.8), kind=kOutput, calls=%fused_computation.17 | convolution fusion | flops 1074003968 | bytes 9961472 | tf_op jit(solution)/shard_map/dot_general | solution.py:107
  235.2 33.1 %reduce-scatter.5.cloned.1.call-done = f32[256,128]{0,1:T(8,128)} async-done(((f32[2048,128]{0,1:T(8,128)}), f32[256,128]{0,1:T(8,128)}) %reduce-scatter.5.cloned.1.call-update) | async-done | bytes 131088 | tf_op jit(solution)/shard_map/reduce_scatter | solution.py:106
  269.2 14.9 %all_gather.29 = bf16[2048,128]{0,1:T(8,128)(2,1)S(1)} all-gather(bf16[256,128]{0,1:T(8,128)(2,1)S(1)} %get-tuple-element.15), channel_id=1, replica_groups=mesh['samp'=4,'var'=8] {'var'}, dimensions={0}, use_global_device_ids=true | all-gather | bytes 589824 | tf_op jit(solution)/shard_map/all_gather | solution.py:113
  284.2 4.7 %fusion = f32[2048,128]{0,1:T(8,128)S(1)} fusion(bf16[2048,128]{0,1:T(8,128)(2,1)S(1)} %all_gather.29, bf16[2048,2048]{1,0:T(8,128)(2,1)} %param.8), kind=kOutput, calls=%fused_computation.15 | convolution fusion | flops 1074003968 | bytes 9961472 | tf_op jit(solution)/shard_map/dot_general | solution.py:115
  290.3 50.9 %all-gather.11.cloned.1.call-done = f32[4,8,4,64,128]{4,3,2,1,0:T(8,128)} async-done(((f32[1,8,4,64,128]{4,3,2,1,0:T(8,128)}), f32[4,8,4,64,128]{4,3,2,1,0:T(8,128)}) %all-gather.11.cloned.1.call-update) | async-done | bytes 4194320 | tf_op jit(solution)/shard_map/all_gather | solution.py:121
  350.3 4.9 %collective-permute-done.15 = bf16[4,64,128]{2,1,0:T(8,128)(2,1)S(1)} collective-permute-done((bf16[4,64,128]{2,1,0:T(8,128)(2,1)S(1)}, bf16[4,64,128]{2,1,0:T(8,128)(2,1)S(1)}, u32[]{:S(2)}, u32[]{:S(2)}) %collective-permute-start.15) | collective-permute-done | bytes 65568 | tf_op jit(solution)/shard_map/ppermute | solution.py:13
  358.5 23.8 %all-gather.13.cloned.1.call-done = bf16[16,4,64,128]{3,2,1,0:T(8,128)(2,1)} async-done(((bf16[16,1,64,128]{3,2,1,0:T(8,128)(2,1)}), bf16[16,4,64,128]{3,2,1,0:T(8,128)(2,1)}) %all-gather.13.cloned.1.call-update) | async-done | bytes 1048592 | tf_op jit(solution)/shard_map/all_gather | solution.py:132
  382.3 4.2 %gather_fusion.11 = bf16[64,256,128]{2,1,0:T(8,128)(2,1)} fusion(bf16[16,256,128]{2,1,0:T(8,128)(2,1)} %bitcast.101, s32[1024]{0:T(1024)S(1)} %pad_clamp_fusion), kind=kCustom, calls=%fused_computation.11 | custom fusion | bytes 8388864 | tf_op jit(solution)/shard_map/gather | solution.py:134
  386.5 6.1 %bitcast_select_fusion = bf16[16,1024,128]{2,1,0:T(8,128)(2,1)S(1)} fusion(pred[16,1024]{1,0:T(8,128)(4,1)S(1)} %bitcast.113, bf16[16,1024,128]{2,1,0:T(8,128)(2,1)} %bitcast.102), kind=kLoop, calls=%fused_computation.12 | loop fusion | flops 2097152 | bytes 8404992 | tf_op jit(solution)/shard_map/jit(_where)/select_n | solution.py:134
  (124 shorter events, 52.6 us)
Async XLA Ops:
  7.2 72.2 %reduce-scatter.3.cloned.1.call-start = ((), (), s32[]{:S(2)}) async-start(), calls=%async_computation.2 | async-start | bytes 1179648 | tf_op jit(solution)/shard_map/reduce_scatter | solution.py:106
  15.9 8.6 %collective-permute-start = (bf16[4,64,128]{2,1,0:T(8,128)(2,1)S(1)}, bf16[4,64,128]{2,1,0:T(8,128)(2,1)S(1)}, u32[]{:S(2)}, u32[]{:S(2)}) collective-permute-start(bf16[4,64,128]{2,1,0:T(8,128)(2,1)S(1)} %get-tuple-element.29), channel_id=1, source_target_pairs={{1,0},{2,1},{3,2},{4,3},{5,4},{6,5},{7,6},{0,7},{9,8},{10,9},{11,1... | collective-permute-start | bytes 196616 | tf_op jit(solution)/shard_map/ppermute | solution.py:13
  20.5 6.6 %collective-permute-start.3 = (bf16[4,64,128]{2,1,0:T(8,128)(2,1)S(1)}, bf16[4,64,128]{2,1,0:T(8,128)(2,1)S(1)}, u32[]{:S(2)}, u32[]{:S(2)}) collective-permute-start(bf16[4,64,128]{2,1,0:T(8,128)(2,1)S(1)} %get-tuple-element.30), channel_id=1, source_target_pairs={{4,0},{5,1},{6,2},{7,3},{0,4},{1,5},{2,6},{3,7},{12,8},{13,9},{14,... | collective-permute-start | bytes 196616 | tf_op jit(solution)/shard_map/ppermute | solution.py:13
  20.5 6.6 %collective-permute-start.2 = (bf16[4,64,128]{2,1,0:T(8,128)(2,1)S(1)}, bf16[4,64,128]{2,1,0:T(8,128)(2,1)S(1)}, u32[]{:S(2)}, u32[]{:S(2)}) collective-permute-start(bf16[4,64,128]{2,1,0:T(8,128)(2,1)S(1)} %get-tuple-element.31), channel_id=1, source_target_pairs={{3,0},{4,1},{5,2},{6,3},{7,4},{0,5},{1,6},{2,7},{11,8},{12,9},{13,... | collective-permute-start | bytes 196616 | tf_op jit(solution)/shard_map/ppermute | solution.py:13
  20.5 6.6 %collective-permute-start.1 = (bf16[4,64,128]{2,1,0:T(8,128)(2,1)S(1)}, bf16[4,64,128]{2,1,0:T(8,128)(2,1)S(1)}, u32[]{:S(2)}, u32[]{:S(2)}) collective-permute-start(bf16[4,64,128]{2,1,0:T(8,128)(2,1)S(1)} %get-tuple-element.32), channel_id=1, source_target_pairs={{2,0},{3,1},{4,2},{5,3},{6,4},{7,5},{0,6},{1,7},{10,8},{11,9},{12,... | collective-permute-start | bytes 196616 | tf_op jit(solution)/shard_map/ppermute | solution.py:13
  39.0 7.4 %copy-start.3 = (f32[256,128]{1,0:T(8,128)S(1)}, f32[256,128]{1,0:T(8,128)}, u32[]{:S(2)}) copy-start(f32[256,128]{1,0:T(8,128)} %param.9) | copy-start | bytes 393220
  46.4 105.9 %all-gather.7.cloned.1.call-start = ((), (), s32[]{:S(2)}) async-start(), calls=%async_computation.3 | async-start | bytes 5242880 | tf_op jit(solution)/shard_map/all_gather | solution.py:121
  101.3 92.1 %all-gather.9.cloned.1.call-start = ((), (), s32[]{:S(2)}) async-start(), calls=%async_computation.4 | async-start | bytes 1310720 | tf_op jit(solution)/shard_map/all_gather | solution.py:132
  155.7 5.7 %collective-permute-start.4 = (bf16[4,64,128]{2,1,0:T(8,128)(2,1)S(1)}, bf16[4,64,128]{2,1,0:T(8,128)(2,1)S(1)}, u32[]{:S(2)}, u32[]{:S(2)}) collective-permute-start(bf16[4,64,128]{2,1,0:T(8,128)(2,1)S(1)} %get-tuple-element.25), channel_id=1, source_target_pairs={{7,0},{0,1},{1,2},{2,3},{3,4},{4,5},{5,6},{6,7},{15,8},{8,9},{9,10... | collective-permute-start | bytes 196616 | tf_op jit(solution)/shard_map/ppermute | solution.py:13
  155.8 10.5 %collective-permute-start.7 = (bf16[4,64,128]{2,1,0:T(8,128)(2,1)S(1)}, bf16[4,64,128]{2,1,0:T(8,128)(2,1)S(1)}, u32[]{:S(2)}, u32[]{:S(2)}) collective-permute-start(bf16[4,64,128]{2,1,0:T(8,128)(2,1)S(1)} %get-tuple-element.26), channel_id=1, source_target_pairs={{4,0},{5,1},{6,2},{7,3},{0,4},{1,5},{2,6},{3,7},{12,8},{13,9},{14,... | collective-permute-start | bytes 196616 | tf_op jit(solution)/shard_map/ppermute | solution.py:13
  158.3 9.1 %collective-permute-start.6 = (bf16[4,64,128]{2,1,0:T(8,128)(2,1)S(1)}, bf16[4,64,128]{2,1,0:T(8,128)(2,1)S(1)}, u32[]{:S(2)}, u32[]{:S(2)}) collective-permute-start(bf16[4,64,128]{2,1,0:T(8,128)(2,1)S(1)} %get-tuple-element.27), channel_id=1, source_target_pairs={{5,0},{6,1},{7,2},{0,3},{1,4},{2,5},{3,6},{4,7},{13,8},{14,9},{15,... | collective-permute-start | bytes 196616 | tf_op jit(solution)/shard_map/ppermute | solution.py:13
  159.6 7.7 %collective-permute-start.5 = (bf16[4,64,128]{2,1,0:T(8,128)(2,1)S(1)}, bf16[4,64,128]{2,1,0:T(8,128)(2,1)S(1)}, u32[]{:S(2)}, u32[]{:S(2)}) collective-permute-start(bf16[4,64,128]{2,1,0:T(8,128)(2,1)S(1)} %get-tuple-element.28), channel_id=1, source_target_pairs={{6,0},{7,1},{0,2},{1,3},{2,4},{3,5},{4,6},{5,7},{14,8},{15,9},{8,1... | collective-permute-start | bytes 196616 | tf_op jit(solution)/shard_map/ppermute | solution.py:13
  168.8 99.5 %reduce-scatter.5.cloned.1.call-start = ((), (), s32[]{:S(2)}) async-start(), calls=%async_computation.5 | async-start | bytes 1179648 | tf_op jit(solution)/shard_map/reduce_scatter | solution.py:106
  197.7 6.2 %copy-start.4 = (f32[128]{0:T(128)S(1)}, f32[128]{0:T(128)}, u32[]{:S(2)}) copy-start(f32[128]{0:T(128)} %param.13) | copy-start | bytes 1540
  206.4 6.2 %collective-permute-start.8 = (bf16[4,64,128]{2,1,0:T(8,128)(2,1)S(1)}, bf16[4,64,128]{2,1,0:T(8,128)(2,1)S(1)}, u32[]{:S(2)}, u32[]{:S(2)}) collective-permute-start(bf16[4,64,128]{2,1,0:T(8,128)(2,1)S(1)} %get-tuple-element.21), channel_id=1, source_target_pairs={{1,0},{2,1},{3,2},{4,3},{5,4},{6,5},{7,6},{0,7},{9,8},{10,9},{11,1... | collective-permute-start | bytes 196616 | tf_op jit(solution)/shard_map/ppermute | solution.py:13
  209.1 6.6 %collective-permute-start.11 = (bf16[4,64,128]{2,1,0:T(8,128)(2,1)S(1)}, bf16[4,64,128]{2,1,0:T(8,128)(2,1)S(1)}, u32[]{:S(2)}, u32[]{:S(2)}) collective-permute-start(bf16[4,64,128]{2,1,0:T(8,128)(2,1)S(1)} %get-tuple-element.22), channel_id=1, source_target_pairs={{4,0},{5,1},{6,2},{7,3},{0,4},{1,5},{2,6},{3,7},{12,8},{13,9},{14,... | collective-permute-start | bytes 196616 | tf_op jit(solution)/shard_map/ppermute | solution.py:13
  209.1 6.6 %collective-permute-start.10 = (bf16[4,64,128]{2,1,0:T(8,128)(2,1)S(1)}, bf16[4,64,128]{2,1,0:T(8,128)(2,1)S(1)}, u32[]{:S(2)}, u32[]{:S(2)}) collective-permute-start(bf16[4,64,128]{2,1,0:T(8,128)(2,1)S(1)} %get-tuple-element.23), channel_id=1, source_target_pairs={{3,0},{4,1},{5,2},{6,3},{7,4},{0,5},{1,6},{2,7},{11,8},{12,9},{13,... | collective-permute-start | bytes 196616 | tf_op jit(solution)/shard_map/ppermute | solution.py:13
  209.2 6.4 %collective-permute-start.9 = (bf16[4,64,128]{2,1,0:T(8,128)(2,1)S(1)}, bf16[4,64,128]{2,1,0:T(8,128)(2,1)S(1)}, u32[]{:S(2)}, u32[]{:S(2)}) collective-permute-start(bf16[4,64,128]{2,1,0:T(8,128)(2,1)S(1)} %get-tuple-element.24), channel_id=1, source_target_pairs={{2,0},{3,1},{4,2},{5,3},{6,4},{7,5},{0,6},{1,7},{10,8},{11,9},{12,... | collective-permute-start | bytes 196616 | tf_op jit(solution)/shard_map/ppermute | solution.py:13
  235.1 106.0 %all-gather.11.cloned.1.call-start = ((), (), s32[]{:S(2)}) async-start(), calls=%async_computation.6 | async-start | bytes 5242880 | tf_op jit(solution)/shard_map/all_gather | solution.py:121
  290.2 92.1 %all-gather.13.cloned.1.call-start = ((), (), s32[]{:S(2)}) async-start(), calls=%async_computation.7 | async-start | bytes 1310720 | tf_op jit(solution)/shard_map/all_gather | solution.py:132
  344.6 5.7 %collective-permute-start.12 = (bf16[4,64,128]{2,1,0:T(8,128)(2,1)S(1)}, bf16[4,64,128]{2,1,0:T(8,128)(2,1)S(1)}, u32[]{:S(2)}, u32[]{:S(2)}) collective-permute-start(bf16[4,64,128]{2,1,0:T(8,128)(2,1)S(1)} %get-tuple-element.17), channel_id=1, source_target_pairs={{7,0},{0,1},{1,2},{2,3},{3,4},{4,5},{5,6},{6,7},{15,8},{8,9},{9,10... | collective-permute-start | bytes 196616 | tf_op jit(solution)/shard_map/ppermute | solution.py:13
  344.7 10.5 %collective-permute-start.15 = (bf16[4,64,128]{2,1,0:T(8,128)(2,1)S(1)}, bf16[4,64,128]{2,1,0:T(8,128)(2,1)S(1)}, u32[]{:S(2)}, u32[]{:S(2)}) collective-permute-start(bf16[4,64,128]{2,1,0:T(8,128)(2,1)S(1)} %get-tuple-element.18), channel_id=1, source_target_pairs={{4,0},{5,1},{6,2},{7,3},{0,4},{1,5},{2,6},{3,7},{12,8},{13,9},{14,... | collective-permute-start | bytes 196616 | tf_op jit(solution)/shard_map/ppermute | solution.py:13
  347.2 9.1 %collective-permute-start.14 = (bf16[4,64,128]{2,1,0:T(8,128)(2,1)S(1)}, bf16[4,64,128]{2,1,0:T(8,128)(2,1)S(1)}, u32[]{:S(2)}, u32[]{:S(2)}) collective-permute-start(bf16[4,64,128]{2,1,0:T(8,128)(2,1)S(1)} %get-tuple-element.19), channel_id=1, source_target_pairs={{5,0},{6,1},{7,2},{0,3},{1,4},{2,5},{3,6},{4,7},{13,8},{14,9},{15,... | collective-permute-start | bytes 196616 | tf_op jit(solution)/shard_map/ppermute | solution.py:13
  348.5 7.7 %collective-permute-start.13 = (bf16[4,64,128]{2,1,0:T(8,128)(2,1)S(1)}, bf16[4,64,128]{2,1,0:T(8,128)(2,1)S(1)}, u32[]{:S(2)}, u32[]{:S(2)}) collective-permute-start(bf16[4,64,128]{2,1,0:T(8,128)(2,1)S(1)} %get-tuple-element.20), channel_id=1, source_target_pairs={{6,0},{7,1},{0,2},{1,3},{2,4},{3,5},{4,6},{5,7},{14,8},{15,9},{8,1... | collective-permute-start | bytes 196616 | tf_op jit(solution)/shard_map/ppermute | solution.py:13
  (3 other events, 18.5 us)
Sparse Core Ops, SparseCore 0:
  46.5 32.8 reduce-scatter.2
  101.4 50.8 all-gather.6
  168.9 24.4 all-gather.8
  235.3 33.0 reduce-scatter.4
  290.3 50.7 all-gather.10
  357.8 24.4 all-gather.12
